TPU v7x, 32 devices: a whole 2x2x4 slice. The times are simulated.
32 devices in a mesh: wide: 8 (over y, x, core), narrow: 4 (over z).
Axes of the slice: x: 2, y: 2, z: 4, core: 2. Of those that a mesh axis runs over, the one named last changes fastest.
Arguments:
- tokens: bfloat16 [16384, 768], P(('wide', 'narrow')), may hold values from -6 to 6
- noise: int32 [16384], P(('wide', 'narrow')), may hold values 0 or 1
- seq_lengths: int32 [8, 4], P('wide'), may hold values from 0 to 2048, as said below
- ln1_gain: float32 [768], replicated, may hold values from 0.25 to 1.75
- ln1_bias: float32 [768], replicated, may hold values from -3 to 3
- qkv_weight: bfloat16 [3, 768, 768], P(None, None, 'narrow'), may hold values from -0.21875 to 0.21875
- out_weight: bfloat16 [768, 768], P('narrow'), may hold values from -3 to 3
- ln2_gain: float32 [768], replicated, may hold values from 0.25 to 1.75
- ln2_bias: float32 [768], replicated, may hold values from -3 to 3
- up_weight: bfloat16 [768, 3072], P(None, 'narrow'), may hold values from -0.21875 to 0.21875
- up_bias: float32 [3072], P('narrow'), may hold values from -4 to 4
- down_weight: bfloat16 [3072, 768], P('narrow'), may hold values from -0.109375 to 0.109375
- down_bias: float32 [768], replicated, may hold values from -3 to 3
- mask_vector: float32 [768], replicated, may hold values from -4 to 4
- cotangent: bfloat16 [2, 16384, 768], P(None, ('wide', 'narrow')), may hold values from -6 to 6
Outputs:
- output: bfloat16 [2, 16384, 768], P(None, ('wide', 'narrow'))
- d_tokens: bfloat16 [16384, 768], P(('wide', 'narrow'))
- d_ln1_gain: float32 [768], replicated
- d_ln1_bias: float32 [768], replicated
- d_qkv_weight: float32 [3, 768, 768], P(None, 'wide', 'narrow')
- d_out_weight: float32 [768, 768], P('narrow', 'wide')
- d_ln2_gain: float32 [768], replicated
- d_ln2_bias: float32 [768], replicated
- d_up_weight: float32 [768, 3072], P('wide', 'narrow')
- d_up_bias: float32 [3072], P(('narrow', 'wide'))
- d_down_weight: float32 [3072, 768], P('narrow', 'wide')
- d_down_bias: float32 [768], replicated
- d_mask_vector: float32 [768], replicated
Inputs may be any that keep to these rules, and one draw needn't show every extreme that they name: `seq_lengths`: row w lists the sequences packed on index w of wide in order; every length is a multiple of 16 and a row sums to 2048. A quarter of the rows hold one sequence of 2048 tokens followed by zeros; the others hold four sequences, each at least 1 token long.
All inputs are finite; a program needn't handle non-finite values. No bound on the sum of `noise` on one device may be relied on, other than what follows from the above.
Results may differ from a plain program's by a relative error of at most 0.019.
Values may be sent and summed in bfloat16 or wider, within the bound.
No kernel may reach another device: no remote copies, remote signals or barrier semaphores. Data moves between devices by JAX's collectives and lax.ppermute only.
A program may use at most 256 MiB of HBM per device.

v0:
```python
import math
import jax
import jax.numpy as jnp
from jax import lax
from jax.sharding import PartitionSpec as P

HEAD = 64
BLOCK = 16
EPS = 1e-05


def layer_norm(values, gain, shift):
    center = values - jnp.mean(values, axis=-1, keepdims=True)
    spread = jnp.mean(center * center, axis=-1, keepdims=True)
    return center * lax.rsqrt(spread + EPS) * gain + shift


def gelu_tanh(values):
    return jax.nn.gelu(values, approximate=True)


def rotate(values, cosines, sines):
    half = values.shape[-1] // 2
    turned = jnp.concatenate([-values[..., half:], values[..., :half]], axis=-1)
    return values * cosines + turned * sines


def angle_tables(positions, head):
    index_f = jnp.arange(head // 2).astype(jnp.float32)
    freqs = jnp.exp(index_f * (-2.0 * math.log(10000.0) / head))
    angles = positions.astype(jnp.float32)[:, None] * freqs[None, :]
    cosines = jnp.concatenate([jnp.cos(angles), jnp.cos(angles)], axis=-1)[:, None, :]
    sines = jnp.concatenate([jnp.sin(angles), jnp.sin(angles)], axis=-1)[:, None, :]
    return (cosines, sines)


def token_meta(lengths_row, count, block):
    ends = jnp.cumsum(lengths_row)
    starts = ends - lengths_row
    places = jnp.arange(count)
    seq_id = jnp.sum((places[:, None] >= ends[None, :]).astype(jnp.int32), axis=1)
    slot_ids = jnp.arange(lengths_row.shape[0])
    first = jnp.sum(jnp.where(seq_id[:, None] == slot_ids[None, :], starts[None, :], 0), axis=1)
    return (seq_id, places - first, places // block)


def allowed_pairs(q_seq, q_blk, q_copy, k_seq, k_blk, k_copy):
    same = q_seq[:, None] == k_seq[None, :]
    q_b = q_blk[:, None]
    k_b = k_blk[None, :]
    q_noisy = q_copy[:, None] == 0
    k_noisy = k_copy[None, :] == 0
    rule = jnp.where(
        q_noisy,
        jnp.where(k_noisy, q_b == k_b, k_b < q_b),
        jnp.logical_and(jnp.logical_not(k_noisy), k_b <= q_b),
    )
    return jnp.logical_and(same, rule)


def inner_rows(left, right):
    return lax.dot_general(
        left, right, (((0,), (0,)), ((), ())), preferred_element_type=jnp.float32
    )


def times_trans(left, right):
    return lax.dot_general(
        left, right, (((1,), (1,)), ((), ())), preferred_element_type=jnp.float32
    )


def per_device(
    tokens,
    noise,
    seq_lengths,
    ln1_gain,
    ln1_bias,
    qkv_weight,
    out_weight,
    ln2_gain,
    ln2_bias,
    up_weight,
    up_bias,
    down_weight,
    down_bias,
    mask_vector,
    cotangent,
):
    f32 = jnp.float32
    bf16 = jnp.bfloat16
    rows_dev, width = tokens.shape
    group_rows = rows_dev * lax.axis_size("narrow")
    count = 2 * group_rows
    local_width = qkv_weight.shape[2]
    heads_dev = local_width // HEAD
    scale = 1.0 / math.sqrt(HEAD)
    width_q = min(512, count)
    count_b = count // width_q
    clean = tokens.astype(f32)
    noisy = jnp.where(noise[:, None] == 1, mask_vector[None, :], clean)
    resid = jnp.stack([noisy, clean])
    normed1, norm1_pull = jax.vjp(layer_norm, resid, ln1_gain, ln1_bias)
    a_all = lax.all_gather(normed1.astype(bf16), "narrow", axis=1, tiled=True).reshape(count, width)
    seq_id, pos, blk = token_meta(seq_lengths[0], group_rows, BLOCK)
    seq2 = jnp.concatenate([seq_id, seq_id])
    pos2 = jnp.concatenate([pos, pos])
    blk2 = jnp.concatenate([blk, blk])
    copy2 = jnp.concatenate(
        [jnp.zeros((group_rows,), jnp.int32), jnp.ones((group_rows,), jnp.int32)]
    )
    cosines, sines = angle_tables(pos2, HEAD)

    def turn(values):
        return rotate(values, cosines, sines)

    q_pre = jnp.dot(a_all, qkv_weight[0], preferred_element_type=f32).reshape(
        count, heads_dev, HEAD
    )
    k_pre = jnp.dot(a_all, qkv_weight[1], preferred_element_type=f32).reshape(
        count, heads_dev, HEAD
    )
    q_rot, q_pull = jax.vjp(turn, q_pre)
    k_rot, k_pull = jax.vjp(turn, k_pre)
    queries = q_rot.astype(bf16)
    keys = k_rot.astype(bf16)
    values = (
        jnp.dot(a_all, qkv_weight[2], preferred_element_type=f32)
        .astype(bf16)
        .reshape(count, heads_dev, HEAD)
    )
    query_blocks = queries.reshape(count_b, width_q, heads_dev, HEAD)
    seq_blocks = seq2.reshape(count_b, width_q)
    blk_blocks = blk2.reshape(count_b, width_q)
    copy_blocks = copy2.reshape(count_b, width_q)

    def forward_block(item):
        q_block, q_seq, q_blk, q_copy = item
        scores = jnp.einsum("qhd,khd->hqk", q_block, keys, preferred_element_type=f32) * scale
        mask = allowed_pairs(q_seq, q_blk, q_copy, seq2, blk2, copy2)
        scores = jnp.where(mask[None], scores, -1e30)
        top = jnp.max(scores, axis=2, keepdims=True)
        lse = top + jnp.log(jnp.sum(jnp.exp(scores - top), axis=2, keepdims=True))
        probs = jnp.exp(scores - lse).astype(bf16)
        return (jnp.einsum("hqk,khd->qhd", probs, values, preferred_element_type=f32), lse[:, :, 0])

    attn_blocks, lse_blocks = lax.map(
        forward_block, (query_blocks, seq_blocks, blk_blocks, copy_blocks)
    )
    attn = attn_blocks.reshape(count, local_width).astype(bf16)
    attn_part = jnp.dot(attn, out_weight, preferred_element_type=f32).reshape(2, group_rows, width)
    attn_out = lax.psum_scatter(
        attn_part.astype(jnp.bfloat16), "narrow", scatter_dimension=1, tiled=True
    ).astype(jnp.float32)
    h_mid = resid + attn_out
    normed2, norm2_pull = jax.vjp(layer_norm, h_mid, ln2_gain, ln2_bias)
    b_all = lax.all_gather(normed2.astype(bf16), "narrow", axis=1, tiled=True).reshape(count, width)
    up_pre = jnp.dot(b_all, up_weight, preferred_element_type=f32) + up_bias
    hidden_f, gelu_pull = jax.vjp(gelu_tanh, up_pre)
    hidden = hidden_f.astype(bf16)
    down_part = jnp.dot(hidden, down_weight, preferred_element_type=f32).reshape(
        2, group_rows, width
    )
    mlp_out = lax.psum_scatter(
        down_part.astype(jnp.bfloat16), "narrow", scatter_dimension=1, tiled=True
    ).astype(jnp.float32)
    output = (h_mid + mlp_out + down_bias).astype(bf16)
    grad_out = cotangent.astype(f32)
    d_down_bias = jnp.sum(grad_out, axis=(0, 1))
    cot_all = lax.all_gather(cotangent, "narrow", axis=1, tiled=True).reshape(count, width)
    d_down = inner_rows(hidden, cot_all)
    d_hidden = times_trans(cot_all, down_weight)
    d_up_low = gelu_pull(d_hidden)[0].astype(bf16)
    d_up = inner_rows(b_all, d_up_low)
    d_up_bias = jnp.sum(d_up_low, axis=0, dtype=f32)
    d_b_part = times_trans(d_up_low, up_weight).reshape(2, group_rows, width)
    d_normed2 = lax.psum_scatter(
        d_b_part.astype(jnp.bfloat16), "narrow", scatter_dimension=1, tiled=True
    ).astype(jnp.float32)
    d_h_ln, d_ln2_gain, d_ln2_bias = norm2_pull(d_normed2)
    d_h_mid = grad_out + d_h_ln
    d_z = d_h_mid.astype(bf16)
    d_z_all = lax.all_gather(d_z, "narrow", axis=1, tiled=True).reshape(count, width)
    d_out = inner_rows(attn, d_z_all)
    d_attn = times_trans(d_z_all, out_weight).astype(bf16)
    d_attn_blocks = d_attn.reshape(count_b, width_q, heads_dev, HEAD)

    def backward_block(carry, item):
        d_keys, d_values = carry
        q_block, lse_block, d_block, q_seq, q_blk, q_copy = item
        scores = jnp.einsum("qhd,khd->hqk", q_block, keys, preferred_element_type=f32) * scale
        mask = allowed_pairs(q_seq, q_blk, q_copy, seq2, blk2, copy2)
        scores = jnp.where(mask[None], scores, -1e30)
        probs = jnp.exp(scores - lse_block[:, :, None])
        d_probs = jnp.einsum("qhd,khd->hqk", d_block, values, preferred_element_type=f32)
        delta = jnp.sum(d_probs * probs, axis=2, keepdims=True)
        d_scores = (probs * (d_probs - delta)).astype(bf16)
        d_query = jnp.einsum("hqk,khd->qhd", d_scores, keys, preferred_element_type=f32) * scale
        d_keys = (
            d_keys
            + jnp.einsum("hqk,qhd->khd", d_scores, q_block, preferred_element_type=f32) * scale
        )
        d_values = d_values + jnp.einsum(
            "hqk,qhd->khd", probs.astype(bf16), d_block, preferred_element_type=f32
        )
        return ((d_keys, d_values), d_query)

    empty = jnp.zeros((count, heads_dev, HEAD), f32)
    (d_keys, d_values), d_query_blocks = lax.scan(
        backward_block,
        (empty, empty),
        (query_blocks, lse_blocks, d_attn_blocks, seq_blocks, blk_blocks, copy_blocks),
    )
    d_q_low = (
        q_pull(d_query_blocks.reshape(count, heads_dev, HEAD))[0]
        .astype(bf16)
        .reshape(count, local_width)
    )
    d_k_low = k_pull(d_keys)[0].astype(bf16).reshape(count, local_width)
    d_v_low = d_values.astype(bf16).reshape(count, local_width)
    d_qkv = jnp.stack(
        [inner_rows(a_all, d_q_low), inner_rows(a_all, d_k_low), inner_rows(a_all, d_v_low)]
    )
    d_a_part = (
        times_trans(d_q_low, qkv_weight[0])
        + times_trans(d_k_low, qkv_weight[1])
        + times_trans(d_v_low, qkv_weight[2])
    ).reshape(2, group_rows, width)
    d_normed1 = lax.psum_scatter(
        d_a_part.astype(jnp.bfloat16), "narrow", scatter_dimension=1, tiled=True
    ).astype(jnp.float32)
    d_resid_ln, d_ln1_gain, d_ln1_bias = norm1_pull(d_normed1)
    d_resid = d_h_mid + d_resid_ln
    masked = noise[:, None] == 1
    d_tokens = (d_resid[1] + jnp.where(masked, 0.0, d_resid[0])).astype(bf16)
    d_mask = jnp.sum(jnp.where(masked, d_resid[0], 0.0), axis=0)
    summed = (
        lax.psum_scatter(d_qkv, "wide", scatter_dimension=1, tiled=True),
        lax.psum_scatter(d_out, "wide", scatter_dimension=1, tiled=True),
        lax.psum_scatter(d_up, "wide", scatter_dimension=0, tiled=True),
        lax.psum_scatter(d_down, "wide", scatter_dimension=1, tiled=True),
        lax.psum_scatter(d_up_bias[None, :], "wide", scatter_dimension=1, tiled=True),
    )
    small = lax.psum(
        (d_ln1_gain, d_ln1_bias, d_ln2_gain, d_ln2_bias, d_down_bias, d_mask), ("wide", "narrow")
    )
    return (
        output,
        d_tokens,
        small[0],
        small[1],
        summed[0],
        summed[1],
        small[2],
        small[3],
        summed[2],
        summed[4][0],
        summed[3],
        small[4],
        small[5],
    )


def solution(mesh):
    placed = (
        P(("wide", "narrow"), None),
        P(("wide", "narrow")),
        P("wide", None),
        P(),
        P(),
        P(None, None, "narrow"),
        P("narrow", None),
        P(),
        P(),
        P(None, "narrow"),
        P("narrow"),
        P("narrow", None),
        P(),
        P(),
        P(None, ("wide", "narrow"), None),
    )
    return jax.shard_map(
        per_device,
        mesh=mesh,
        in_specs=placed,
        out_specs=(
            P(None, ("wide", "narrow"), None),
            P(("wide", "narrow"), None),
            P(),
            P(),
            P(None, "wide", "narrow"),
            P("narrow", "wide"),
            P(),
            P(),
            P("wide", "narrow"),
            P(("narrow", "wide")),
            P("narrow", "wide"),
            P(),
            P(),
        ),
        check_vma=False,
    )
```

profile of v0, /device:TPU:0, one launch (start us, length us, event | category | flops | bytes accessed | tf_op | source)
XLA Modules:
  0.0 2366.9 jit_solution(2762413686105143079)
XLA Ops:
  20.2 113.0 %all-gather.5.cloned.1.call-done = bf16[2,2048,768]{2,1,0:T(8,128)(2,1)} async-done(((bf16[2,512,768]{2,1,0:T(8,128)(2,1)}), bf16[2,2048,768]{2,1,0:T(8,128)(2,1)}) %all-gather.5.cloned.1.call-update) | async-done | bytes 6291472 | tf_op jit(solution)/shard_map/all_gather | solution.py:104
  148.6 346.6 %while.27 = (s32[]{:T(128)}, bf16[8,512,3,64]{1,3,2,0:T(8,128)(2,1)}, f32[8,3,512]{2,1,0:T(4,128)}, s32[8,512]{1,0:T(8,128)}, s32[4096]{0:T(1024)S(1)}, /*index=...) while((s32[]{:T(128)}, ...), condition=%wide.region_8.9_spmd, body=%wide.region_5.8_spmd.sunk | while | flops 1696594944 | bytes 94020792 | solution.py:147
  508.9 109.1 %reduce-scatter.16.cloned.1.call-done = bf16[2,512,768]{2,1,0:T(8,128)(2,1)} async-done(((bf16[2,2048,768]{2,1,0:T(8,128)(2,1)}), bf16[2,512,768]{2,1,0:T(8,128)(2,1)}) %reduce-scatter.16.cloned.1.call-update) | async-done | bytes 1572880 | tf_op jit(solution)/shard_map/reduce_scatter | solution.py:152
  624.9 115.4 %all-gather.7.cloned.1.call-done = bf16[2,2048,768]{2,1,0:T(8,128)(2,1)} async-done(((bf16[2,512,768]{2,1,0:T(8,128)(2,1)}), bf16[2,2048,768]{2,1,0:T(8,128)(2,1)}) %all-gather.7.cloned.1.call-update) | async-done | bytes 6291472 | tf_op jit(solution)/shard_map/all_gather | solution.py:157
  750.8 104.4 %all-gather.9.cloned.1.call-done = bf16[2,2048,768]{2,1,0:T(8,128)(2,1)} async-done(((bf16[2,512,768]{2,1,0:T(8,128)(2,1)}), bf16[2,2048,768]{2,1,0:T(8,128)(2,1)}) %all-gather.9.cloned.1.call-update) | async-done | bytes 6291472 | tf_op jit(solution)/shard_map/all_gather | solution.py:170
  855.2 18.5 convert_reduce_fusion
  880.8 109.1 %reduce-scatter.20.cloned.1.call-done = bf16[2,512,768]{2,1,0:T(8,128)(2,1)} async-done(((bf16[2,2048,768]{2,1,0:T(8,128)(2,1)}), bf16[2,512,768]{2,1,0:T(8,128)(2,1)}) %reduce-scatter.20.cloned.1.call-update) | async-done | bytes 1572880 | tf_op jit(solution)/shard_map/reduce_scatter | solution.py:177
  1003.5 111.3 %all-gather.11.cloned.1.call-done = bf16[2,2048,768]{2,1,0:T(8,128)(2,1)} async-done(((bf16[2,512,768]{2,1,0:T(8,128)(2,1)}), bf16[2,2048,768]{2,1,0:T(8,128)(2,1)}) %all-gather.11.cloned.1.call-update) | async-done | bytes 6291472 | tf_op jit(solution)/shard_map/all_gather | solution.py:183
  1128.3 818.9 %while.28 = (s32[]{:T(128)}, f32[4096,3,64]{0,2,1:T(8,128)}, f32[4096,3,64]{0,2,1:T(8,128)}, f32[8,512,3,64]{1,0,3,2:T(8,128)}, bf16[8,512,3,64]{1,3,2,0:T(8,128...) while((s32[]{:T(128)}, f32[4096,3,64]{0,2,1:T(8,128)}, ...), condition=%wide.region_18.19_spmd.clone, body=%wide.region_16.18_spmd.clone.sunk | while | flops 4141710336 | bytes 229868800 | solution.py:209
  1162.4 18.2 multiply_reduce_fusion.4
  1180.6 21.7 multiply_convert_fusion.3
  1250.1 13.8 fusion.166
  1264.0 18.2 multiply_reduce_fusion.4
  1282.2 21.7 multiply_convert_fusion.3
  1352.6 13.8 fusion.166
  1366.4 18.2 multiply_reduce_fusion.4
  1384.6 21.7 multiply_convert_fusion.3
  1455.1 13.8 fusion.166
  1468.9 18.2 multiply_reduce_fusion.4
  1487.1 21.7 multiply_convert_fusion.3
  1571.4 18.2 multiply_reduce_fusion.4
  1589.6 21.7 multiply_convert_fusion.3
  1673.9 18.2 multiply_reduce_fusion.4
  1692.1 21.7 multiply_convert_fusion.3
  1776.4 18.2 multiply_reduce_fusion.4
  1794.6 21.7 multiply_convert_fusion.3
  1878.9 18.2 multiply_reduce_fusion.4
  1897.1 21.7 multiply_convert_fusion.3
  2050.2 103.0 %reduce-scatter.22.cloned.1.call-done = bf16[2,512,768]{2,1,0:T(8,128)(2,1)} async-done(((bf16[2,2048,768]{2,1,0:T(8,128)(2,1)}), bf16[2,512,768]{2,1,0:T(8,128)(2,1)}) %reduce-scatter.22.cloned.1.call-update) | async-done | bytes 1572880 | tf_op jit(solution)/shard_map/reduce_scatter | solution.py:229
  2158.3 108.6 %reduce-scatter.18.cloned.1.call-done = bf16[2,512,768]{2,1,0:T(8,128)(2,1)} async-done(((bf16[2,2048,768]{2,1,0:T(8,128)(2,1)}), bf16[2,512,768]{2,1,0:T(8,128)(2,1)}) %reduce-scatter.18.cloned.1.call-update) | async-done | bytes 1572880 | tf_op jit(solution)/shard_map/reduce_scatter | solution.py:164
  2275.0 41.5 %all-reduce.4 = (f32[768]{0:T(1024)}, f32[768]{0:T(1024)}, f32[768]{0:T(1024)}, f32[768]{0:T(1024)}, f32[768]{0:T(1024)}, /*index=5*/f32[768]{0:T(1024)}) all-reduce(f32[768]{0:T(1024)S(1)} %get-tuple-element.328, f32[768]{0:T(1024)S(1)} %get-tuple-element.332, ...), channel_id=1, replica_groups=mesh['wide'=8,'narrow'=4] {'wide','narrow'}, use_global_device_ids=true, to_apply=%region_23.24 | all-reduce | flops 4608 | bytes 36864 | tf_op jit(solution)/shard_map/psum | solution.py:244
  2316.5 43.7 %reduce-scatter.26.cloned.1.call-done = f32[768,96]{0,1:T(8,128)} async-done(((f32[768,768]{0,1:T(8,128)}), f32[768,96]{0,1:T(8,128)}) %reduce-scatter.26.cloned.1.call-update) | async-done | bytes 294928 | tf_op jit(solution)/shard_map/reduce_scatter | solution.py:241
  (409 shorter events, 1012.7 us)
Async XLA Ops:
  7.2 848.0 %copy-start = (bf16[768,768]{1,0:T(8,128)(2,1)S(1)}, bf16[768,768]{1,0:T(8,128)(2,1)}, u32[]{:S(2)}) copy-start(bf16[768,768]{1,0:T(8,128)(2,1)} %param.30) | copy-start | bytes 3538948
  7.2 126.0 %all-gather.5.cloned.1.call-start = ((), (), s32[]{:S(2)}) async-start(), calls=%async_computation.9 | async-start | bytes 7864320 | tf_op jit(solution)/shard_map/all_gather | solution.py:104
  15.0 603.0 %reduce-scatter.16.cloned.1.call-start = ((), (), s32[]{:S(2)}) async-start(), calls=%async_computation.10 | async-start | bytes 7864320 | tf_op jit(solution)/shard_map/reduce_scatter | solution.py:152
  508.8 231.4 %all-gather.7.cloned.1.call-start = ((), (), s32[]{:S(2)}) async-start(), calls=%async_computation.11 | async-start | bytes 7864320 | tf_op jit(solution)/shard_map/all_gather | solution.py:157
  620.7 375.8 %copy-start.27 = (f32[2,512]{1,0:T(2,128)}, f32[2,512]{1,0:T(2,128)S(1)}, u32[]{:S(2)}) copy-start(f32[2,512]{1,0:T(2,128)S(1)} %broadcast_multiply_fusion.2) | copy-start | bytes 12292
  622.5 374.0 %copy-start.33 = (f32[2,512]{1,0:T(2,128)}, f32[2,512]{1,0:T(2,128)S(1)}, u32[]{:S(2)}) copy-start(f32[2,512]{1,0:T(2,128)S(1)} %fusion.81) | copy-start | bytes 12292
  624.2 231.0 %all-gather.9.cloned.1.call-start = ((), (), s32[]{:S(2)}) async-start(), calls=%async_computation.13 | async-start | bytes 7864320 | tf_op jit(solution)/shard_map/all_gather | solution.py:170
  624.8 365.1 %reduce-scatter.20.cloned.1.call-start = ((), (), s32[]{:S(2)}) async-start(), calls=%async_computation.14 | async-start | bytes 7864320 | tf_op jit(solution)/shard_map/reduce_scatter | solution.py:177
  740.2 115.0 %copy-start.55 = (f32[768]{0:T(1024)S(1)}, f32[768]{0:T(1024)}, u32[]{:S(2)}) copy-start(f32[768]{0:T(1024)} %param.29) | copy-start | bytes 9220
  880.8 234.0 %all-gather.11.cloned.1.call-start = ((), (), s32[]{:S(2)}) async-start(), calls=%async_computation.15 | async-start | bytes 7864320 | tf_op jit(solution)/shard_map/all_gather | solution.py:183
  998.8 1046.3 %reduce-scatter.32.cloned.1.call-start = ((), (), s32[]{:S(2)}) async-start(), calls=%async_computation.21 | async-start | bytes 442368
  1003.4 1043.1 %reduce-scatter.30.cloned.1.call-start = ((), (), s32[]{:S(2)}) async-start(), calls=%async_computation.20 | async-start | bytes 884736
  1312.8 19.0 copy-start.3
  1415.3 19.0 copy-start.3
  1517.8 19.0 copy-start.3
  1963.4 84.8 %reduce-scatter.28.cloned.1.call-start = ((), (), s32[]{:S(2)}) async-start(), calls=%async_computation.19 | async-start | bytes 2211840
  1986.4 166.9 %reduce-scatter.22.cloned.1.call-start = ((), (), s32[]{:S(2)}) async-start(), calls=%async_computation.16 | async-start | bytes 7864320 | tf_op jit(solution)/shard_map/reduce_scatter | solution.py:229
  2014.6 252.3 %reduce-scatter.18.cloned.1.call-start = ((), (), s32[]{:S(2)}) async-start(), calls=%async_computation.12 | async-start | bytes 7864320 | tf_op jit(solution)/shard_map/reduce_scatter | solution.py:164
  2024.3 292.1 %reduce-scatter.24.cloned.1.call-start = ((), (), s32[]{:S(2)}) async-start(), calls=%async_computation.17 | async-start | bytes 2654208 | tf_op jit(solution)/shard_map/reduce_scatter | solution.py:240
  2034.6 325.5 %reduce-scatter.26.cloned.1.call-start = ((), (), s32[]{:S(2)}) async-start(), calls=%async_computation.18 | async-start | bytes 2654208 | tf_op jit(solution)/shard_map/reduce_scatter | solution.py:241
  2045.0 108.3 %copy-start.7 = (f32[1,512,768]{2,1,0:T(8,128)S(1)}, f32[1,512,768]{2,1,0:T(8,128)}, u32[]{:S(2)}) copy-start(f32[1,512,768]{2,1,0:T(8,128)} %copy-done.6) | copy-start | bytes 4718596
  2045.0 108.3 %copy-start.30 = (f32[2,512]{1,0:T(2,128)S(1)}, f32[2,512]{1,0:T(2,128)}, u32[]{:S(2)}) copy-start(f32[2,512]{1,0:T(2,128)} %copy-done.29) | copy-start | bytes 12292
  2045.0 108.3 %copy-start.38 = (f32[768]{0:T(1024)S(1)}, f32[768]{0:T(1024)}, u32[]{:S(2)}) copy-start(f32[768]{0:T(1024)} %param.22) | copy-start | bytes 9220
  2045.1 111.4 %copy-start.44 = (f32[2,512]{1,0:T(2,128)S(1)}, f32[2,512]{1,0:T(2,128)}, u32[]{:S(2)}) copy-start(f32[2,512]{1,0:T(2,128)} %copy-done.43) | copy-start | bytes 12292
  2046.6 109.9 %copy-start.40 = (f32[2,512]{1,0:T(2,128)S(1)}, f32[2,512]{1,0:T(2,128)}, u32[]{:S(2)}) copy-start(f32[2,512]{1,0:T(2,128)} %copy-done.39) | copy-start | bytes 12292
  2156.4 110.5 %copy-start.28 = (f32[2,512]{1,0:T(2,128)S(1)}, f32[2,512]{1,0:T(2,128)}, u32[]{:S(2)}) copy-start(f32[2,512]{1,0:T(2,128)} %copy-done.27) | copy-start | bytes 12292
  2156.4 110.5 %copy-start.32 = (f32[768]{0:T(1024)S(1)}, f32[768]{0:T(1024)}, u32[]{:S(2)}) copy-start(f32[768]{0:T(1024)} %param.26) | copy-start | bytes 9220
  2156.4 110.5 %copy-start.34 = (f32[2,512]{1,0:T(2,128)S(1)}, f32[2,512]{1,0:T(2,128)}, u32[]{:S(2)}) copy-start(f32[2,512]{1,0:T(2,128)} %copy-done.33) | copy-start | bytes 12292
  2156.4 110.5 %copy-start.36 = (f32[2,512]{1,0:T(2,128)S(1)}, f32[2,512]{1,0:T(2,128)}, u32[]{:S(2)}) copy-start(f32[2,512]{1,0:T(2,128)} %copy-done.35) | copy-start | bytes 12292
  2156.4 110.5 %copy-start.42 = (f32[2,512]{1,0:T(2,128)S(1)}, f32[2,512]{1,0:T(2,128)}, u32[]{:S(2)}) copy-start(f32[2,512]{1,0:T(2,128)} %copy-done.41) | copy-start | bytes 12292
  2156.5 110.5 %copy-start.51 = (f32[768]{0:T(1024)S(1)}, f32[768]{0:T(1024)}, u32[]{:S(2)}) copy-start(f32[768]{0:T(1024)} %param.31) | copy-start | bytes 9220
  2158.3 115.5 %copy-start.48 = (pred[512]{0:T(512)(128)(4,1)S(1)}, pred[512]{0:T(512)(128)(4,1)}, u32[]{:S(2)}) copy-start(pred[512]{0:T(512)(128)(4,1)} %copy-done.47) | copy-start | bytes 1540
  (62 other events, 376.7 us)
Sparse Core Ops, SparseCore 0:
  15.1 118.0 all-gather.4
  509.0 108.9 reduce-scatter.15
  624.4 115.8 all-gather.6
  741.7 113.5 all-gather.8
  880.9 108.9 reduce-scatter.19
  998.9 115.8 all-gather.10
  1117.8 32.0 reduce-scatter.31
  1963.5 33.0 reduce-scatter.29
  2000.1 40.1 reduce-scatter.27
  2042.5 110.7 reduce-scatter.21
  2155.6 111.2 reduce-scatter.17
  2270.7 42.9 reduce-scatter.23
  2317.6 42.4 reduce-scatter.25
where the time goes:
time: 2380 us; the launch traced here: 2370 us
  waiting for transfers between devices  918 us (39%)
  matrix products  833 us (35%)
  other arithmetic  427 us (18%)
  local copies, waits for them, and re-layouts  130 us (5%)
  blocking collectives  41.5 us (2%)
    convert_element_type x8, other arithmetic, backward_block(): d_scores = (probs * (d_probs - delta)).astype(bf16)  174 us
    dot_general x8, matrix products, backward_block(): jnp.einsum('qhd,khd->hqk', d_block, values, preferred_element_type=f32)  146 us
    all_gather x1, waiting for transfers between devices, per_device(): lax.all_gather(normed2.astype(bf16), 'narrow', axis=1, tiled=True)  115 us
    all_gather x1, waiting for transfers between devices, per_device(): lax.all_gather(normed1.astype(bf16), 'narrow', axis=1, tiled=True)  113 us
    all_gather x1, waiting for transfers between devices, per_device(): lax.all_gather(d_z, 'narrow', axis=1, tiled=True).reshape(count, width)  111 us
    dot_general x8, matrix products, backward_block(): jnp.einsum('hqk,qhd->khd', probs.astype(bf16), d_block, preferred_element...  110 us
    reduce_scatter x1, waiting for transfers between devices, per_device(): lax.psum_scatter(attn_part.astype(jnp.bfloat16), 'narrow', scatter_dimens...  109 us
    reduce_scatter x1, waiting for transfers between devices, per_device(): lax.psum_scatter(d_b_part.astype(jnp.bfloat16), 'narrow', scatter_dimensi...  109 us
  transfers between devices with their start and end apart: 13, of which 9 were waited for; matrix products, arithmetic and copies ran while one was open for 41% of the time, Pallas kernels for 0%

commit v1 on v0

--- a/solution.py
+++ b/solution.py
@@ -1,12 +1,48 @@
+import functools
 import math
 import jax
 import jax.numpy as jnp
 from jax import lax
 from jax.sharding import PartitionSpec as P
+from jax.lax import axis_index, ppermute, psum
 
 HEAD = 64
 BLOCK = 16
 EPS = 1e-05
+
+
+def store_units_on(row_data, dimension_no):
+    right_arr = psum(1, axis_name="narrow")
+    y_new = axis_index("narrow")
+    opened, later, all_values = (right_arr, y_new, row_data.shape[dimension_no])
+    v1 = range(opened)
+    s_next = map(lambda j: (j, (j + 1) % opened), v1)
+    queue = list(s_next)
+    g_now = map(lambda j: (j, (j - 1) % opened), range(opened))
+    heard = jnp.zeros(
+        (*row_data.shape[:dimension_no], opened * all_values, *row_data.shape[dimension_no + 1 :]),
+        row_data.dtype,
+    )
+    heard = lax.dynamic_update_slice_in_dim(heard, row_data, later * all_values, axis=dimension_no)
+    frames = list(g_now)
+    work_now = current_value = row_data
+    it = 1
+    current_arr = opened // 2
+    while it < current_arr + 1:
+        work_now = ppermute(work_now, axis_name="narrow", perm=queue)
+        heard = lax.dynamic_update_slice_in_dim(
+            heard, work_now, (later - it) % opened * all_values, axis=dimension_no
+        )
+        if it < opened - current_arr:
+            current_value = ppermute(current_value, axis_name="narrow", perm=frames)
+            heard = lax.dynamic_update_slice_in_dim(
+                heard, current_value, (later + it) % opened * all_values, axis=dimension_no
+            )
+        it += 1
+    return heard
+
+
+match_sources_all_for = functools.partial(store_units_on, dimension_no=1)
 
 
 def layer_norm(values, gain, shift):
@@ -167,7 +203,7 @@
     output = (h_mid + mlp_out + down_bias).astype(bf16)
     grad_out = cotangent.astype(f32)
     d_down_bias = jnp.sum(grad_out, axis=(0, 1))
-    cot_all = lax.all_gather(cotangent, "narrow", axis=1, tiled=True).reshape(count, width)
+    cot_all = match_sources_all_for(cotangent).reshape(count, width)
     d_down = inner_rows(hidden, cot_all)
     d_hidden = times_trans(cot_all, down_weight)
     d_up_low = gelu_pull(d_hidden)[0].astype(bf16)

time: 2380 us -> 2370 us (level)
  waiting for transfers between devices: 918 us -> 832 us
  starting transfers between devices: 1.39 us -> 65.2 us
    ppermute x0 -> x3, waiting for transfers between devices: none -> 125 us  [the longest x2 109 us: store_units_on(): work_now = ppermute(work_now, axis_name='narrow', perm=queue)]
    all_gather x1, waiting for transfers between devices: 115 us -> 5.84 us  [per_device(): lax.all_gather(normed2.astype(bf16), 'narrow', axis=1, tiled=True)]
    all_gather x1 -> x0, waiting for transfers between devices: 104 us -> none  [per_device(): lax.all_gather(cotangent, 'narrow', axis=1, tiled=True)]
    ppermute x0 -> x3, starting transfers between devices: none -> 63.9 us  [the longest x2 61.6 us: store_units_on(): work_now = ppermute(work_now, axis_name='narrow', perm=queue)]
  transfers between devices with their start and end apart: 13 -> 15, of which waited for: 9 -> 11; matrix products, arithmetic and copies ran while one was open for 41% -> 41% of each run, Pallas kernels for 0% -> 0%
where the time goes in v1:
time: 2370 us; the launch traced here: 2360 us
  matrix products  834 us (35%)
  waiting for transfers between devices  832 us (35%)
  other arithmetic  427 us (18%)
  local copies, waits for them, and re-layouts  142 us (6%)
  starting transfers between devices  65.2 us (3%)
  blocking collectives  41.4 us (2%)
    convert_element_type x8, other arithmetic, backward_block(): d_scores = (probs * (d_probs - delta)).astype(bf16)  174 us
    dot_general x8, matrix products, backward_block(): jnp.einsum('qhd,khd->hqk', d_block, values, preferred_element_type=f32)  146 us
    all_gather x1, waiting for transfers between devices, per_device(): lax.all_gather(normed1.astype(bf16), 'narrow', axis=1, tiled=True)  113 us
    reduce_scatter x1, waiting for transfers between devices, per_device(): lax.psum_scatter(d_b_part.astype(jnp.bfloat16), 'narrow', scatter_dimensi...  112 us
    all_gather x1, waiting for transfers between devices, per_device(): lax.all_gather(d_z, 'narrow', axis=1, tiled=True).reshape(count, width)  111 us
    dot_general x8, matrix products, backward_block(): jnp.einsum('hqk,qhd->khd', probs.astype(bf16), d_block, preferred_element...  111 us
    ppermute x2, waiting for transfers between devices, store_units_on(): work_now = ppermute(work_now, axis_name='narrow', perm=queue)  109 us
    reduce_scatter x1, waiting for transfers between devices, per_device(): lax.psum_scatter(attn_part.astype(jnp.bfloat16), 'narrow', scatter_dimens...  109 us
  transfers between devices with their start and end apart: 15, of which 11 were waited for; matrix products, arithmetic and copies ran while one was open for 41% of the time, Pallas kernels for 0%

profile of v1, /device:TPU:0, one launch (start us, length us, event | category | flops | bytes accessed | tf_op | source)
XLA Modules:
  0.0 2358.4 jit_solution(6969092854187254237)
XLA Ops:
  20.2 113.0 %all-gather.4.cloned.1.call-done = bf16[2,2048,768]{2,1,0:T(8,128)(2,1)} async-done(((bf16[2,512,768]{2,1,0:T(8,128)(2,1)}), bf16[2,2048,768]{2,1,0:T(8,128)(2,1)}) %all-gather.4.cloned.1.call-update) | async-done | bytes 6291472 | tf_op jit(solution)/shard_map/all_gather | solution.py:140
  148.6 347.0 %while.27 = (s32[]{:T(128)}, bf16[8,512,3,64]{1,3,2,0:T(8,128)(2,1)}, f32[8,3,512]{2,1,0:T(4,128)}, s32[8,512]{1,0:T(8,128)}, s32[4096]{0:T(1024)S(1)}, /*index=...) while((s32[]{:T(128)}, ...), condition=%wide.region_8.9_spmd, body=%wide.region_5.8_spmd.sunk | while | flops 1696594944 | bytes 94020792 | solution.py:183
  509.3 109.1 %reduce-scatter.16.cloned.1.call-done = bf16[2,512,768]{2,1,0:T(8,128)(2,1)} async-done(((bf16[2,2048,768]{2,1,0:T(8,128)(2,1)}), bf16[2,512,768]{2,1,0:T(8,128)(2,1)}) %reduce-scatter.16.cloned.1.call-update) | async-done | bytes 1572880 | tf_op jit(solution)/shard_map/reduce_scatter | solution.py:188
  628.6 60.9 %collective-permute-done = bf16[2,512,768]{2,1,0:T(8,128)(2,1)} collective-permute-done((bf16[2,512,768]{2,1,0:T(8,128)(2,1)}, bf16[2,512,768]{2,1,0:T(8,128)(2,1)}, u32[]{:S(2)}, u32[]{:S(2)}) %collective-permute-start) | collective-permute-done | bytes 1572896 | tf_op jit(solution)/shard_map/ppermute | solution.py:32
  689.5 60.0 %collective-permute-start.2 = (bf16[2,512,768]{2,1,0:T(8,128)(2,1)}, bf16[2,512,768]{2,1,0:T(8,128)(2,1)}, u32[]{:S(2)}, u32[]{:S(2)}) collective-permute-start(bf16[2,512,768]{2,1,0:T(8,128)(2,1)} %collective-permute-done), channel_id=1, source_target_pairs={{0,1},{1,2},{2,3},{3,0},{4,5},{5,6},{6,7},{7,4},{8,9},{9,10},{10,1... | collective-permute-start | bytes 4718600 | tf_op jit(solution)/shard_map/ppermute | solution.py:32
  756.5 15.6 collective-permute-done.1
  774.9 48.3 %collective-permute-done.2 = bf16[2,512,768]{2,1,0:T(8,128)(2,1)} collective-permute-done((bf16[2,512,768]{2,1,0:T(8,128)(2,1)}, bf16[2,512,768]{2,1,0:T(8,128)(2,1)}, u32[]{:S(2)}, u32[]{:S(2)}) %collective-permute-start.2) | collective-permute-done | bytes 1572896 | tf_op jit(solution)/shard_map/ppermute | solution.py:32
  842.0 18.4 convert_reduce_fusion
  867.6 112.1 %reduce-scatter.20.cloned.1.call-done = bf16[2,512,768]{2,1,0:T(8,128)(2,1)} async-done(((bf16[2,2048,768]{2,1,0:T(8,128)(2,1)}), bf16[2,512,768]{2,1,0:T(8,128)(2,1)}) %reduce-scatter.20.cloned.1.call-update) | async-done | bytes 1572880 | tf_op jit(solution)/shard_map/reduce_scatter | solution.py:213
  993.2 111.3 %all-gather.8.cloned.1.call-done = bf16[2,2048,768]{2,1,0:T(8,128)(2,1)} async-done(((bf16[2,512,768]{2,1,0:T(8,128)(2,1)}), bf16[2,2048,768]{2,1,0:T(8,128)(2,1)}) %all-gather.8.cloned.1.call-update) | async-done | bytes 6291472 | tf_op jit(solution)/shard_map/all_gather | solution.py:219
  1118.0 820.2 %while.28 = (s32[]{:T(128)}, f32[4096,3,64]{0,2,1:T(8,128)}, f32[4096,3,64]{0,2,1:T(8,128)}, f32[8,512,3,64]{1,0,3,2:T(8,128)}, bf16[8,512,3,64]{1,3,2,0:T(8,128...) while((s32[]{:T(128)}, f32[4096,3,64]{0,2,1:T(8,128)}, ...), condition=%wide.region_18.19_spmd.clone, body=%wide.region_16.18_spmd.clone.sunk | while | flops 4141710336 | bytes 229868800 | solution.py:245
  1152.2 18.2 multiply_reduce_fusion.4
  1170.4 21.8 multiply_convert_fusion.3
  1254.0 18.2 multiply_reduce_fusion.4
  1272.2 21.8 multiply_convert_fusion.3
  1356.6 18.2 multiply_reduce_fusion.4
  1374.8 21.8 multiply_convert_fusion.3
  1459.3 18.2 multiply_reduce_fusion.4
  1477.5 21.8 multiply_convert_fusion.3
  1561.9 18.2 multiply_reduce_fusion.4
  1580.1 21.8 multiply_convert_fusion.3
  1650.6 13.9 fusion.166
  1664.6 18.2 multiply_reduce_fusion.4
  1682.8 21.8 multiply_convert_fusion.3
  1767.2 18.2 multiply_reduce_fusion.4
  1785.4 21.8 multiply_convert_fusion.3
  1869.9 18.3 multiply_reduce_fusion.4
  1888.1 21.8 multiply_convert_fusion.3
  2041.1 103.4 %reduce-scatter.22.cloned.1.call-done = bf16[2,512,768]{2,1,0:T(8,128)(2,1)} async-done(((bf16[2,2048,768]{2,1,0:T(8,128)(2,1)}), bf16[2,512,768]{2,1,0:T(8,128)(2,1)}) %reduce-scatter.22.cloned.1.call-update) | async-done | bytes 1572880 | tf_op jit(solution)/shard_map/reduce_scatter | solution.py:265
  2149.6 108.4 %reduce-scatter.18.cloned.1.call-done = bf16[2,512,768]{2,1,0:T(8,128)(2,1)} async-done(((bf16[2,2048,768]{2,1,0:T(8,128)(2,1)}), bf16[2,512,768]{2,1,0:T(8,128)(2,1)}) %reduce-scatter.18.cloned.1.call-update) | async-done | bytes 1572880 | tf_op jit(solution)/shard_map/reduce_scatter | solution.py:200
  2266.1 41.4 %all-reduce.4 = (f32[768]{0:T(1024)}, f32[768]{0:T(1024)}, f32[768]{0:T(1024)}, f32[768]{0:T(1024)}, f32[768]{0:T(1024)}, /*index=5*/f32[768]{0:T(1024)}) all-reduce(f32[768]{0:T(1024)S(1)} %get-tuple-element.328, f32[768]{0:T(1024)S(1)} %get-tuple-element.332, ...), channel_id=1, replica_groups=mesh['wide'=8,'narrow'=4] {'wide','narrow'}, use_global_device_ids=true, to_apply=%region_23.24 | all-reduce | flops 4608 | bytes 36864 | tf_op jit(solution)/shard_map/psum | solution.py:280
  2307.5 43.8 %reduce-scatter.26.cloned.1.call-done = f32[768,96]{0,1:T(8,128)} async-done(((f32[768,768]{0,1:T(8,128)}), f32[768,96]{0,1:T(8,128)}) %reduce-scatter.26.cloned.1.call-update) | async-done | bytes 294928 | tf_op jit(solution)/shard_map/reduce_scatter | solution.py:277
  (419 shorter events, 1062.8 us)
Async XLA Ops:
  7.2 834.8 %copy-start = (bf16[768,768]{1,0:T(8,128)(2,1)S(1)}, bf16[768,768]{1,0:T(8,128)(2,1)}, u32[]{:S(2)}) copy-start(bf16[768,768]{1,0:T(8,128)(2,1)} %param.30) | copy-start | bytes 3538948
  7.2 126.0 %all-gather.4.cloned.1.call-start = ((), (), s32[]{:S(2)}) async-start(), calls=%async_computation.9 | async-start | bytes 7864320 | tf_op jit(solution)/shard_map/all_gather | solution.py:140
  15.0 603.4 %reduce-scatter.16.cloned.1.call-start = ((), (), s32[]{:S(2)}) async-start(), calls=%async_computation.10 | async-start | bytes 7864320 | tf_op jit(solution)/shard_map/reduce_scatter | solution.py:188
  509.3 322.5 %all-gather.6.cloned.1.call-start = ((), (), s32[]{:S(2)}) async-start(), calls=%async_computation.11 | async-start | bytes 7864320 | tf_op jit(solution)/shard_map/all_gather | solution.py:193
  621.2 365.1 %copy-start.28 = (f32[2,512]{1,0:T(2,128)}, f32[2,512]{1,0:T(2,128)S(1)}, u32[]{:S(2)}) copy-start(f32[2,512]{1,0:T(2,128)S(1)} %broadcast_multiply_fusion.2) | copy-start | bytes 12292
  622.9 363.3 %copy-start.34 = (f32[2,512]{1,0:T(2,128)}, f32[2,512]{1,0:T(2,128)S(1)}, u32[]{:S(2)}) copy-start(f32[2,512]{1,0:T(2,128)S(1)} %fusion.81) | copy-start | bytes 12292
  624.7 355.0 %reduce-scatter.20.cloned.1.call-start = ((), (), s32[]{:S(2)}) async-start(), calls=%async_computation.13 | async-start | bytes 7864320 | tf_op jit(solution)/shard_map/reduce_scatter | solution.py:213
  624.7 64.8 %collective-permute-start = (bf16[2,512,768]{2,1,0:T(8,128)(2,1)}, bf16[2,512,768]{2,1,0:T(8,128)(2,1)}, u32[]{:S(2)}, u32[]{:S(2)}) collective-permute-start(bf16[2,512,768]{2,1,0:T(8,128)(2,1)} %param.33), channel_id=1, source_target_pairs={{0,1},{1,2},{2,3},{3,0},{4,5},{5,6},{6,7},{7,4},{8,9},{9,10},{10,1... | collective-permute-start | bytes 4718600 | tf_op jit(solution)/shard_map/ppermute | solution.py:32
  626.3 145.9 %collective-permute-start.1 = (bf16[2,512,768]{2,1,0:T(8,128)(2,1)}, bf16[2,512,768]{2,1,0:T(8,128)(2,1)}, u32[]{:S(2)}, u32[]{:S(2)}) collective-permute-start(bf16[2,512,768]{2,1,0:T(8,128)(2,1)} %param.33), channel_id=1, source_target_pairs={{0,3},{1,0},{2,1},{3,2},{4,7},{5,4},{6,5},{7,6},{8,11},{9,8},{10,9... | collective-permute-start | bytes 4718600 | tf_op jit(solution)/shard_map/ppermute | solution.py:37
  689.5 133.7 %collective-permute-start.2 = (bf16[2,512,768]{2,1,0:T(8,128)(2,1)}, bf16[2,512,768]{2,1,0:T(8,128)(2,1)}, u32[]{:S(2)}, u32[]{:S(2)}) collective-permute-start(bf16[2,512,768]{2,1,0:T(8,128)(2,1)} %collective-permute-done), channel_id=1, source_target_pairs={{0,1},{1,2},{2,3},{3,0},{4,5},{5,6},{6,7},{7,4},{8,9},{9,10},{10,1... | collective-permute-start | bytes 4718600 | tf_op jit(solution)/shard_map/ppermute | solution.py:32
  867.5 237.0 %all-gather.8.cloned.1.call-start = ((), (), s32[]{:S(2)}) async-start(), calls=%async_computation.14 | async-start | bytes 7864320 | tf_op jit(solution)/shard_map/all_gather | solution.py:219
  988.5 1047.5 %reduce-scatter.32.cloned.1.call-start = ((), (), s32[]{:S(2)}) async-start(), calls=%async_computation.20 | async-start | bytes 442368
  993.2 1044.3 %reduce-scatter.30.cloned.1.call-start = ((), (), s32[]{:S(2)}) async-start(), calls=%async_computation.19 | async-start | bytes 884736
  1302.9 19.0 copy-start.3
  1508.2 19.0 copy-start.3
  1954.5 84.6 %reduce-scatter.28.cloned.1.call-start = ((), (), s32[]{:S(2)}) async-start(), calls=%async_computation.18 | async-start | bytes 2211840
  1977.4 167.1 %reduce-scatter.22.cloned.1.call-start = ((), (), s32[]{:S(2)}) async-start(), calls=%async_computation.15 | async-start | bytes 7864320 | tf_op jit(solution)/shard_map/reduce_scatter | solution.py:265
  2005.5 252.5 %reduce-scatter.18.cloned.1.call-start = ((), (), s32[]{:S(2)}) async-start(), calls=%async_computation.12 | async-start | bytes 7864320 | tf_op jit(solution)/shard_map/reduce_scatter | solution.py:200
  2015.2 292.3 %reduce-scatter.24.cloned.1.call-start = ((), (), s32[]{:S(2)}) async-start(), calls=%async_computation.16 | async-start | bytes 2654208 | tf_op jit(solution)/shard_map/reduce_scatter | solution.py:276
  2025.5 325.8 %reduce-scatter.26.cloned.1.call-start = ((), (), s32[]{:S(2)}) async-start(), calls=%async_computation.17 | async-start | bytes 2654208 | tf_op jit(solution)/shard_map/reduce_scatter | solution.py:277
  2035.9 108.6 %copy-start.7 = (f32[1,512,768]{2,1,0:T(8,128)S(1)}, f32[1,512,768]{2,1,0:T(8,128)}, u32[]{:S(2)}) copy-start(f32[1,512,768]{2,1,0:T(8,128)} %copy-done.6) | copy-start | bytes 4718596
  2035.9 108.6 %copy-start.31 = (f32[2,512]{1,0:T(2,128)S(1)}, f32[2,512]{1,0:T(2,128)}, u32[]{:S(2)}) copy-start(f32[2,512]{1,0:T(2,128)} %copy-done.30) | copy-start | bytes 12292
  2035.9 108.6 %copy-start.39 = (f32[768]{0:T(1024)S(1)}, f32[768]{0:T(1024)}, u32[]{:S(2)}) copy-start(f32[768]{0:T(1024)} %param.22) | copy-start | bytes 9220
  2036.0 111.7 %copy-start.45 = (f32[2,512]{1,0:T(2,128)S(1)}, f32[2,512]{1,0:T(2,128)}, u32[]{:S(2)}) copy-start(f32[2,512]{1,0:T(2,128)} %copy-done.44) | copy-start | bytes 12292
  2037.5 110.3 %copy-start.41 = (f32[2,512]{1,0:T(2,128)S(1)}, f32[2,512]{1,0:T(2,128)}, u32[]{:S(2)}) copy-start(f32[2,512]{1,0:T(2,128)} %copy-done.40) | copy-start | bytes 12292
  2147.6 110.3 %copy-start.29 = (f32[2,512]{1,0:T(2,128)S(1)}, f32[2,512]{1,0:T(2,128)}, u32[]{:S(2)}) copy-start(f32[2,512]{1,0:T(2,128)} %copy-done.28) | copy-start | bytes 12292
  2147.6 110.3 %copy-start.33 = (f32[768]{0:T(1024)S(1)}, f32[768]{0:T(1024)}, u32[]{:S(2)}) copy-start(f32[768]{0:T(1024)} %param.26) | copy-start | bytes 9220
  2147.7 110.3 %copy-start.35 = (f32[2,512]{1,0:T(2,128)S(1)}, f32[2,512]{1,0:T(2,128)}, u32[]{:S(2)}) copy-start(f32[2,512]{1,0:T(2,128)} %copy-done.34) | copy-start | bytes 12292
  2147.7 110.3 %copy-start.37 = (f32[2,512]{1,0:T(2,128)S(1)}, f32[2,512]{1,0:T(2,128)}, u32[]{:S(2)}) copy-start(f32[2,512]{1,0:T(2,128)} %copy-done.36) | copy-start | bytes 12292
  2147.7 110.3 %copy-start.43 = (f32[2,512]{1,0:T(2,128)S(1)}, f32[2,512]{1,0:T(2,128)}, u32[]{:S(2)}) copy-start(f32[2,512]{1,0:T(2,128)} %copy-done.42) | copy-start | bytes 12292
  2147.7 110.3 %copy-start.52 = (f32[768]{0:T(1024)S(1)}, f32[768]{0:T(1024)}, u32[]{:S(2)}) copy-start(f32[768]{0:T(1024)} %param.31) | copy-start | bytes 9220
  2149.6 115.3 %copy-start.49 = (pred[512]{0:T(512)(128)(4,1)S(1)}, pred[512]{0:T(512)(128)(4,1)}, u32[]{:S(2)}) copy-start(pred[512]{0:T(512)(128)(4,1)} %copy-done.48) | copy-start | bytes 1540
  (65 other events, 409.2 us)
Sparse Core Ops, SparseCore 0:
  15.1 118.0 all-gather.3
  509.4 108.9 reduce-scatter.15
  624.8 206.8 all-gather.5
  867.6 111.9 reduce-scatter.19
  988.6 115.8 all-gather.7
  1107.4 32.0 reduce-scatter.31
  1954.6 33.0 reduce-scatter.29
  1991.2 40.1 reduce-scatter.27
  2033.7 110.7 reduce-scatter.21
  2146.7 111.2 reduce-scatter.17
  2261.9 42.9 reduce-scatter.23
  2308.6 42.6 reduce-scatter.25
